TPU v7x, 32 devices: a whole 2x2x4 slice. The times are simulated.
32 devices in a mesh: groups: 2 (over y), seq: 4 (over z), dp: 4 (over x, core).
Axes of the slice: x: 2, y: 2, z: 4, core: 2. Of those that a mesh axis runs over, the one named last changes fastest.
Arguments:
- inputs: bfloat16 [8, 32768, 768], P(('groups', 'dp'), 'seq'), parts along dimension 0, may hold values from -33 to 33, as said below
- norm_gain: float32 [768], replicated, may hold values from 0.5 to 1.5
- inner_mix: bfloat16 [256, 256], replicated, may hold values from -0.375 to 0.375
- twiddle: float32 [128, 256], P('seq'), may hold values from 0.5 to 2
- outer_mix: bfloat16 [128, 128], replicated, may hold values from -0.5 to 0.5
- long_kernel: float32 [128, 256], P(None, 'seq'), may hold values from 0.5 to 2
- gate_weight: bfloat16 [768, 384], replicated, may hold values from -0.3125 to 0.3125
- out_weight: bfloat16 [768, 384], replicated, may hold values from -0.3125 to 0.3125
- cotangent: bfloat16 [8, 32768, 768], P(('groups', 'dp'), 'seq'), parts along dimension 0, may hold values from -6 to 6
Outputs:
- layer_out: bfloat16 [8, 32768, 768], P(('groups', 'dp'), 'seq'), parts along dimension 0
- input_grad: bfloat16 [8, 32768, 768], P(('groups', 'dp'), 'seq'), parts along dimension 0
- weight_grads: float32 [3072, 384], P(('groups', 'seq')), parts along dimension 0
There are 2 independent parts, one for each index of `groups`. A program takes and returns all parts, laid end to end along the dimension named above; an argument that names none is the same for every part. Nothing has to cross between parts.
Inputs may be any that keep to these rules, and one draw needn't show every extreme that they name: `inputs`: activations' entries.
All inputs are finite; a program needn't handle non-finite values.
Results may differ from a plain program's by a relative error of at most 0.0072.
Values may be sent and summed in bfloat16 or wider, within the bound.
A program may use at most 384 MiB of HBM per device.

v0:
```python
import math

import jax
import jax.numpy as jnp
from jax import lax
from jax.sharding import PartitionSpec as P

norm_eps = 1e-06


def normalize(values, norm_gain):
    mean_square = jnp.mean(values * values, axis=-1, keepdims=True)
    return values * lax.rsqrt(mean_square + norm_eps) * norm_gain


def block_apply(operand, weight):
    blocks = weight.shape[0] // weight.shape[1]
    grouped = operand.reshape(operand.shape[0], blocks, weight.shape[1])
    stacked = weight.reshape(blocks, weight.shape[1], weight.shape[1])
    result = jnp.einsum("rki,kij->rkj", grouped, stacked, preferred_element_type=jnp.float32)
    return result.reshape(operand.shape[0], -1)


def block_back(partner, weight):
    blocks = weight.shape[0] // weight.shape[1]
    grouped = partner.reshape(partner.shape[0], blocks, weight.shape[1])
    stacked = weight.reshape(blocks, weight.shape[1], weight.shape[1])
    result = jnp.einsum("rkj,kij->rki", grouped, stacked, preferred_element_type=jnp.float32)
    return result.reshape(partner.shape[0], -1)


def block_term(operand, partner, blocks, block_size):
    grouped = operand.reshape(operand.shape[0], blocks, block_size)
    other_rows = partner.reshape(partner.shape[0], blocks, block_size)
    result = jnp.einsum("rki,rkj->kij", grouped, other_rows, preferred_element_type=jnp.float32)
    return result.reshape(blocks * block_size, block_size)


def to_columns(row_layout):
    return lax.all_to_all(row_layout, "seq", split_axis=2, concat_axis=1, tiled=True)


def to_rows(col_layout):
    return lax.all_to_all(col_layout, "seq", split_axis=1, concat_axis=2, tiled=True)


def shards(
    inputs,
    norm_gain,
    inner_mix,
    twiddle,
    outer_mix,
    long_kernel,
    gate_weight,
    out_weight,
    cotangent,
):
    batch_local, rows_local, channels = inputs.shape
    inner_len = inner_mix.shape[0]
    local_outer = rows_local // inner_len
    flat_rows = batch_local * rows_local
    block_size = gate_weight.shape[1]
    blocks = gate_weight.shape[0] // block_size
    all_tokens = batch_local * lax.axis_size("dp") * rows_local * lax.axis_size("seq")
    grad_scale = 1.0 / math.sqrt(all_tokens)
    inputs_wide = inputs.reshape(flat_rows, channels).astype(jnp.float32)
    activation = normalize(inputs_wide, norm_gain).astype(jnp.bfloat16)
    grid_rows = activation.reshape(batch_local, local_outer, inner_len, channels)
    inner_out = jnp.einsum(
        "jq,bpqd->bpjd", inner_mix, grid_rows, preferred_element_type=jnp.float32
    )
    mixed_rows = (inner_out * twiddle[None, :, :, None]).astype(jnp.bfloat16)
    columns = to_columns(mixed_rows)
    outer_out = jnp.einsum("ip,bpjd->bijd", outer_mix, columns, preferred_element_type=jnp.float32)
    mixed_cols = (outer_out * long_kernel[None, :, :, None]).astype(jnp.bfloat16)
    seq_mix = to_rows(mixed_cols).reshape(flat_rows, channels)
    gate_pre = block_apply(activation, gate_weight)
    gate_sig = jax.nn.sigmoid(gate_pre)
    mix_wide = seq_mix.astype(jnp.float32)
    gated_rows = (mix_wide * gate_pre * gate_sig).astype(jnp.bfloat16)
    layer_out = (inputs_wide + block_apply(gated_rows, out_weight)).astype(jnp.bfloat16)
    cotan_rows = cotangent.reshape(flat_rows, channels)
    back_gated = block_back(cotan_rows, out_weight)
    mix_grad = (back_gated * gate_pre * gate_sig).astype(jnp.bfloat16)
    gate_grad = (back_gated * mix_wide * gate_sig * (1.0 + gate_pre * (1.0 - gate_sig))).astype(
        jnp.bfloat16
    )
    act_grad = block_back(gate_grad, gate_weight)
    weight_term = jnp.concatenate(
        [
            block_term(activation, gate_grad, blocks, block_size),
            block_term(gated_rows, cotan_rows, blocks, block_size),
        ],
        axis=0,
    )
    grad_cols = to_columns(mix_grad.reshape(batch_local, local_outer, inner_len, channels))
    scaled_back = (grad_cols.astype(jnp.float32) * long_kernel[None, :, :, None]).astype(
        jnp.bfloat16
    )
    back_outer = jnp.einsum(
        "ip,bijd->bpjd", outer_mix, scaled_back, preferred_element_type=jnp.float32
    ).astype(jnp.bfloat16)
    back_rows = to_rows(back_outer)
    twisted = (back_rows.astype(jnp.float32) * twiddle[None, :, :, None]).astype(jnp.bfloat16)
    inner_back = jnp.einsum("jq,bpjd->bpqd", inner_mix, twisted, preferred_element_type=jnp.float32)
    act_grad = act_grad + inner_back.reshape(flat_rows, channels)
    pullback = jax.vjp(lambda wide_rows: normalize(wide_rows, norm_gain), inputs_wide)[1]
    input_grad = (cotan_rows.astype(jnp.float32) + pullback(act_grad)[0]).astype(jnp.bfloat16)
    shard_term = lax.psum_scatter(weight_term, "seq", scatter_dimension=0, tiled=True)
    weight_grads = lax.psum(shard_term, "dp") * grad_scale
    return (layer_out.reshape(inputs.shape), input_grad.reshape(inputs.shape), weight_grads)


def solution(mesh):
    return jax.shard_map(
        shards,
        mesh=mesh,
        in_specs=(
            P(("groups", "dp"), "seq", None),
            P(),
            P(),
            P("seq", None),
            P(),
            P(None, "seq"),
            P(),
            P(),
            P(("groups", "dp"), "seq", None),
        ),
        out_specs=(
            P(("groups", "dp"), "seq", None),
            P(("groups", "dp"), "seq", None),
            P(("groups", "seq"), None),
        ),
        check_vma=False,
    )
```

profile of v0, /device:TPU:21, one launch (start us, length us, event | category | flops | bytes accessed | tf_op | source)
XLA Modules:
  0.0 1638.3 jit_solution(11999235351812838798)
XLA Ops:
  28.8 24.7 %copy.107 = f32[32,256,768]{1,2,0:T(8,128)} copy(f32[32,256,768]{2,1,0:T(8,128)} %bitcast.156) | data formatting | bytes 50331648 | tf_op jit(solution)/shard_map/convert_element_type | solution.py:66
  67.6 16.6 %copy.108 = bf16[1,32,256,768]{3,1,0,2:T(8,128)(2,1)} copy(bf16[1,32,256,768]{2,3,1,0:T(8,128)(2,1)} %fusion.24) | data formatting | bytes 25165824 | tf_op jit(solution)/shard_map/convert_element_type | solution.py:72
  84.2 275.7 %all_to_all.42 = bf16[1,32,256,768]{3,1,0,2:T(8,128)(2,1)S(1)} all-to-all(bf16[1,32,256,768]{3,1,0,2:T(8,128)(2,1)} %copy.108), channel_id=1, replica_groups=mesh['groups'=2,'seq'=4,'dp'=4] {'seq'}, dimensions={2} | all-to-all | bytes 25165824 | tf_op jit(solution)/shard_map/all_to_all | solution.py:40
  359.9 16.4 %copy.109 = bf16[1,32,256,768]{3,2,1,0:T(8,128)(2,1)S(1)} copy(bf16[1,32,256,768]{3,1,0,2:T(8,128)(2,1)S(1)} %all_to_all.42) | data formatting | bytes 25165824 | tf_op jit(solution)/shard_map/all_to_all | solution.py:40
  381.6 24.2 %fusion.7 = bf16[1,128,64,768]{1,3,2,0:T(8,128)(2,1)} fusion(f32[128,64]{0,1:T(8,128)S(1)} %copy-done.12, bf16[128,64,768]{2,1,0:T(8,128)(2,1)} %bitcast.157, bf16[128,128]{1,0:T(8,128)(2,1)S(1)} %copy-done.16), kind=kOutput, calls=%fused_computation.14 | convolution fusion | flops 1623195648 | bytes 25231360 | tf_op jit(solution)/shard_map/ip,bpjd->bijd/dot_general | solution.py:74
  405.8 16.5 %copy.112 = bf16[1,128,64,768]{3,2,0,1:T(8,128)(2,1)} copy(bf16[1,128,64,768]{1,3,2,0:T(8,128)(2,1)} %fusion.7) | data formatting | bytes 25165824 | tf_op jit(solution)/shard_map/convert_element_type | solution.py:75
  430.4 17.6 %copy.142 = f32[1,8192,768]{1,2,0:T(8,128)} copy(bf16[1,8192,768]{2,1,0:T(8,128)(2,1)} %param.9) | data formatting | bytes 37748736 | tf_op jit(solution)/shard_map/convert_element_type | solution.py:66
  448.0 24.3 %reshape_reshape.4 = bf16[8192,2,384]{2,1,0:T(2,128)(2,1)} reshape(bf16[1,8192,768]{2,1,0:T(8,128)(2,1)} %param.17) | data formatting | bytes 25165824 | tf_op jit(solution)/shard_map/reshape;reshape | solution.py:26
  472.4 21.1 %fusion.41 = f32[2,8192,384]{2,1,0:T(8,128)} fusion(bf16[2,384,384]{2,1,0:T(8,128)(2,1)S(1)} %bitcast.163, f32[8192,2,384]{0,2,1:T(8,128)} %bitcast.152, f32[2,384]{1,0:T(2,128)S(1)} %mul.196, f32[8192]{0:T(1024)S(1)} %fusion.46), kind=kOutput, calls=%fused_computation.57 | convolution fusion | flops 4850712576 | bytes 50957312 | tf_op jit(solution)/shard_map/rki,kij->rkj/dot_general | solution.py:20
  493.5 206.3 %all-to-all-done.1 = bf16[1,128,64,768]{3,2,0,1:T(8,128)(2,1)} async-done(((bf16[1,128,64,768]{3,2,0,1:T(8,128)(2,1)}), bf16[1,128,64,768]{3,2,0,1:T(8,128)(2,1)}, u32[]{:S(2)}, u32[]{:S(2)}) %all-to-all-start.1) | async-done | bytes 12582944 | tf_op jit(solution)/shard_map/all_to_all | solution.py:44
  716.6 30.3 %reshape.272 = f32[8192,2,384]{2,1,0:T(2,128)} reshape(f32[1,32,4,64,768]{4,3,2,1,0:T(8,128)} %copy.114) | data formatting | bytes 50331648 | tf_op jit(solution)/shard_map/convert_element_type | solution.py:79
  746.9 39.9 %fusion.13 = (bf16[8192,2,384]{2,0,1:T(8,128)(2,1)}, bf16[8192,2,384]{2,0,1:T(8,128)(2,1)}, bf16[8192,2,384]{2,0,1:T(8,128)(2,1)}) fusion(f32[2,8192,384]{2,1,0:T(8,128)} %fusion.41, f32[8192,2,384]{2,1,0:T(2,128)} %reshape.272, bf16[2,384,384]{2,1,0:T(8,128)(2,1)S(1)} %bitcast.149, bf16[8192,2,384]{2,1,0:T(2,128)(2,1)} %reshape_reshape.4), kind=kOutput, calls=%fused_computation.23 | convolution fusion | flops 4932501504 | bytes 101253120 | tf_op jit(solution)/shard_map/rkj,kij->rki/dot_general | solution.py:28
  786.8 16.2 copy.123
  814.9 18.3 %copy.124 = bf16[1,32,256,768]{3,1,0,2:T(8,128)(2,1)} copy(bf16[1,32,256,768]{2,1,3,0:T(8,128)(2,1)} %bitcast.160) | data formatting | bytes 25165824 | tf_op jit(solution)/shard_map/convert_element_type | solution.py:84
  842.8 269.4 %all-to-all-done.2 = bf16[1,32,256,768]{3,1,0,2:T(8,128)(2,1)} async-done(((bf16[1,32,256,768]{3,1,0,2:T(8,128)(2,1)}), bf16[1,32,256,768]{3,1,0,2:T(8,128)(2,1)}, u32[]{:S(2)}, u32[]{:S(2)}) %all-to-all-start.2) | async-done | bytes 12582944 | tf_op jit(solution)/shard_map/all_to_all | solution.py:40
  1146.6 22.8 %convert_bitcast_fusion.3 = bf16[1,128,64,768]{1,3,2,0:T(8,128)(2,1)} fusion(bf16[128,64,768]{2,1,0:T(8,128)(2,1)} %fusion.8, bf16[128,128]{1,0:T(8,128)(2,1)S(1)} %copy-done.17), kind=kOutput, calls=%fused_computation.49 | convolution fusion | flops 1616904192 | bytes 25198592 | tf_op jit(solution)/shard_map/ip,bijd->bpjd/dot_general | solution.py:100
  1169.4 16.7 %copy.129 = bf16[1,128,64,768]{3,2,0,1:T(8,128)(2,1)} copy(bf16[1,128,64,768]{1,3,2,0:T(8,128)(2,1)} %convert_bitcast_fusion.3) | data formatting | bytes 25165824 | tf_op jit(solution)/shard_map/convert_element_type | solution.py:102
  1209.5 15.7 fusion.40
  1241.5 204.8 %reduce-scatter.2.cloned.1.call-done = f32[384,384]{1,0:T(8,128)} async-done(((f32[1536,384]{1,0:T(8,128)}), f32[384,384]{1,0:T(8,128)}) %reduce-scatter.2.cloned.1.call-update) | async-done | bytes 589840 | tf_op jit(solution)/shard_map/reduce_scatter | solution.py:109
  1460.9 24.8 %copy.134 = f32[8192,768]{1,0:T(8,128)} copy(f32[8192,768]{0,1:T(8,128)} %bitcast.150) | data formatting | bytes 50331648 | tf_op jit(solution)/shard_map/reshape | solution.py:29
  1485.7 24.7 %copy.133 = f32[1,8192,768]{2,1,0:T(8,128)} copy(f32[1,8192,768]{1,2,0:T(8,128)} %bitcast.151) | data formatting | bytes 50331648 | tf_op jit(solution)/shard_map/reshape | solution.py:29
  1510.4 24.7 %copy.119 = f32[1,8192,768]{2,1,0:T(8,128)} copy(f32[1,8192,768]{1,2,0:T(8,128)} %bitcast.155) | data formatting | bytes 50331648 | tf_op jit(solution)/shard_map/reshape | solution.py:21
  1569.3 20.7 %fusion.4 = f32[8192]{0:T(1024)S(1)} fusion(f32[8192,768]{1,0:T(8,128)} %copy.134, f32[32,768,256]{1,2,0:T(8,128)} %fusion.23, bf16[1,8192,768]{2,1,0:T(8,128)(2,1)} %param.9, f32[768]{0:T(1024)S(1)} %copy-done.19), kind=kLoop, calls=%fused_computation.6 | loop fusion | flops 31449088 | bytes 62950400 | tf_op jit(solution)/shard_map/transpose(jvp())/reduce_sum | solution.py:13
  1590.0 41.1 %fusion.1 = (bf16[1,8192,768]{2,1,0:T(8,128)(2,1)}, bf16[1,8192,768]{2,1,0:T(8,128)(2,1)}) fusion(f32[1,8192,768]{2,1,0:T(8,128)} %copy.133, f32[32,768,256]{1,2,0:T(8,128)} %fusion.23, bf16[1,8192,768]{2,1,0:T(8,128)(2,1)} %param.17, bf16[1,8192,768]{2,1,0:T(8,128)(2,1)} %param.9, f32[8192]{0:T(1024)S(1)} %multiply_multiply_fusion, f32[8192]{0:T(1024)S(1)} %copy-done.3, ...), kind=kLoop, calls=%fused_computation.2 | loop fusion | flops 75497472 | bytes 125897728 | tf_op jit(solution)/shard_map/convert_element_type | solution.py:108
  (73 shorter events, 210.2 us)
Async XLA Ops:
  7.2 739.7 %copy-start = (bf16[768,384]{1,0:T(8,128)(2,1)S(1)}, bf16[768,384]{1,0:T(8,128)(2,1)}, u32[]{:S(2)}) copy-start(bf16[768,384]{1,0:T(8,128)(2,1)} %param.16) | copy-start | bytes 1769476
  14.4 14.4 copy-start.10
  28.7 443.7 %copy-start.1 = (f32[8192]{0:T(1024)}, f32[8192]{0:T(1024)S(1)}, u32[]{:S(2)}) copy-start(f32[8192]{0:T(1024)S(1)} %fusion.46) | copy-start | bytes 98308
  28.7 24.8 %copy-start.6 = (f32[32,256]{1,0:T(8,128)S(1)}, f32[32,256]{1,0:T(8,128)}, u32[]{:S(2)}) copy-start(f32[32,256]{1,0:T(8,128)} %param.12) | copy-start | bytes 98308
  28.7 24.8 %copy-start.8 = (bf16[256,256]{1,0:T(8,128)(2,1)S(1)}, bf16[256,256]{1,0:T(8,128)(2,1)}, u32[]{:S(2)}) copy-start(bf16[256,256]{1,0:T(8,128)(2,1)} %param.11) | copy-start | bytes 393220
  28.7 24.7 %copy-start.18 = (f32[768]{0:T(1024)S(1)}, f32[768]{0:T(1024)}, u32[]{:S(2)}) copy-start(f32[768]{0:T(1024)} %param.10) | copy-start | bytes 9220
  359.9 21.7 %copy-start.12 = (f32[128,64]{0,1:T(8,128)S(1)}, f32[128,64]{0,1:T(8,128)}, u32[]{:S(2)}) copy-start(f32[128,64]{0,1:T(8,128)} %param.14) | copy-start | bytes 98308
  359.9 21.7 %copy-start.16 = (bf16[128,128]{1,0:T(8,128)(2,1)S(1)}, bf16[128,128]{1,0:T(8,128)(2,1)}, u32[]{:S(2)}) copy-start(bf16[128,128]{1,0:T(8,128)(2,1)} %param.13) | copy-start | bytes 98308
  422.3 277.5 %all-to-all-start.1 = ((bf16[1,128,64,768]{3,2,0,1:T(8,128)(2,1)}), bf16[1,128,64,768]{3,2,0,1:T(8,128)(2,1)}, u32[]{:S(2)}, u32[]{:S(2)}) async-start(bf16[1,128,64,768]{3,2,0,1:T(8,128)(2,1)} %copy.112), calls=%async_computation.1 | async-start | bytes 25165824 | tf_op jit(solution)/shard_map/all_to_all | solution.py:44
  430.3 42.0 %copy-start.14 = (f32[2,384]{1,0:T(2,128)}, f32[2,384]{1,0:T(2,128)S(1)}, u32[]{:S(2)}) copy-start(f32[2,384]{1,0:T(2,128)S(1)} %mul.196) | copy-start | bytes 9220
  430.3 42.0 %copy-start.4 = (bf16[768,384]{1,0:T(8,128)(2,1)S(1)}, bf16[768,384]{1,0:T(8,128)(2,1)}, u32[]{:S(2)}) copy-start(bf16[768,384]{1,0:T(8,128)(2,1)} %param.15) | copy-start | bytes 1769476
  814.9 27.8 %copy-start.13 = (f32[128,64]{0,1:T(8,128)S(1)}, f32[128,64]{0,1:T(8,128)}, u32[]{:S(2)}) copy-start(f32[128,64]{0,1:T(8,128)} %param.14) | copy-start | bytes 98308
  833.1 279.0 %all-to-all-start.2 = ((bf16[1,32,256,768]{3,1,0,2:T(8,128)(2,1)}), bf16[1,32,256,768]{3,1,0,2:T(8,128)(2,1)}, u32[]{:S(2)}, u32[]{:S(2)}) async-start(bf16[1,32,256,768]{3,1,0,2:T(8,128)(2,1)} %copy.124), calls=%async_computation.2 | async-start | bytes 25165824 | tf_op jit(solution)/shard_map/all_to_all | solution.py:40
  1186.1 350.9 %all-to-all-start.3 = ((bf16[1,128,64,768]{3,2,0,1:T(8,128)(2,1)}), bf16[1,128,64,768]{3,2,0,1:T(8,128)(2,1)}, u32[]{:S(2)}, u32[]{:S(2)}) async-start(bf16[1,128,64,768]{3,2,0,1:T(8,128)(2,1)} %copy.129), calls=%async_computation.3 | async-start | bytes 25165824 | tf_op jit(solution)/shard_map/all_to_all | solution.py:44
  1195.5 250.7 %reduce-scatter.2.cloned.1.call-start = ((), (), s32[]{:S(2)}) async-start(), calls=%async_computation.5 | async-start | bytes 2949120 | tf_op jit(solution)/shard_map/reduce_scatter | solution.py:109
  1195.5 14.0 copy-start.2
  1195.5 14.0 copy-start.15
  1209.5 17.4 %copy-start.5 = (bf16[768,384]{1,0:T(8,128)(2,1)S(1)}, bf16[768,384]{1,0:T(8,128)(2,1)}, u32[]{:S(2)}) copy-start(bf16[768,384]{1,0:T(8,128)(2,1)} %param.15) | copy-start | bytes 1769476
  1226.8 308.3 %all-reduce.2.cloned.1.call-start = ((), (), s32[]{:S(2)}) async-start(), calls=%async_computation.6 | async-start | bytes 1179648 | tf_op jit(solution)/shard_map/psum | solution.py:110
  1544.5 9.3 copy-start.7
  1544.5 9.3 copy-start.9
  1553.8 15.5 copy-start.19
  1569.3 20.7 %copy-start.11 = (f32[8192]{0:T(1024)S(1)}, f32[8192]{0:T(1024)}, u32[]{:S(2)}) copy-start(f32[8192]{0:T(1024)} %copy-done.10) | copy-start | bytes 98308
  1569.3 20.7 %copy-start.3 = (f32[8192]{0:T(1024)S(1)}, f32[8192]{0:T(1024)}, u32[]{:S(2)}) copy-start(f32[8192]{0:T(1024)} %copy-done.1) | copy-start | bytes 98308
  (1 other events, 6.1 us)
Sparse Core Ops, SparseCore 0:
  1226.9 219.3 reduce-scatter.1
  1448.6 32.5 all-reduce.1
where the time goes:
time: 1650 us; the launch traced here: 1640 us
  waiting for transfers between devices  680 us (41%)
  local copies, waits for them, and re-layouts  327 us (20%)
  blocking collectives  276 us (17%)
  matrix products  197 us (12%)
  other arithmetic  117 us (7%)
  starting transfers between devices  27 us (2%)
    all_to_all x1, blocking collectives, to_columns(): lax.all_to_all(row_layout, 'seq', split_axis=2, concat_axis=1, tiled=True)  276 us
    all_to_all x1, waiting for transfers between devices, to_columns(): lax.all_to_all(row_layout, 'seq', split_axis=2, concat_axis=1, tiled=True)  269 us
    all_to_all x2, waiting for transfers between devices, to_rows(): lax.all_to_all(col_layout, 'seq', split_axis=1, concat_axis=2, tiled=True)  206 us
    reduce_scatter x1, waiting for transfers between devices, shards(): lax.psum_scatter(weight_term, 'seq', scatter_dimension=0, tiled=True)  205 us
    dot_general x2, matrix products, block_back(): jnp.einsum('rkj,kij->rki', grouped, stacked, preferred_element_type=jnp.f...  54.5 us
    reshape x2, local copies, waits for them, and re-layouts, block_back(): return result.reshape(partner.shape[0], -1)  49.5 us
    convert_element_type x2, local copies, waits for them, and re-layouts, shards(): inputs_wide = inputs.reshape(flat_rows, channels).astype(jnp.float32)  42.4 us
    convert_element_type x1, other arithmetic, shards(): (cotan_rows.astype(jnp.float32) + pullback(act_grad)[0]).astype(jnp.bfloa...  41.1 us
  transfers between devices with their start and end apart: 5, of which 3 were waited for; matrix products, arithmetic and copies ran while one was open for 12% of the time, Pallas kernels for 0%

commit v1 on v0

--- a/solution.py
+++ b/solution.py
@@ -1,8 +1,11 @@
+import functools
 import math
 
 import jax
 import jax.numpy as jnp
 from jax import lax
+from jax.experimental import pallas as pl
+from jax.experimental.pallas import tpu as pltpu
 from jax.sharding import PartitionSpec as P
 
 norm_eps = 1e-06
@@ -44,7 +47,7 @@
     return lax.all_to_all(col_layout, "seq", split_axis=1, concat_axis=2, tiled=True)
 
 
-def shards(
+def shards_plain(
     inputs,
     norm_gain,
     inner_mix,
@@ -111,6 +114,251 @@
     return (layer_out.reshape(inputs.shape), input_grad.reshape(inputs.shape), weight_grads)
 
 
+def dot(lhs, rhs, lhs_dim=1, rhs_dim=0):
+    return lax.dot_general(
+        lhs, rhs, (((lhs_dim,), (rhs_dim,)), ((), ())), preferred_element_type=jnp.float32
+    )
+
+
+def row_scale(wide, channels):
+    return lax.rsqrt(jnp.sum(wide * wide, axis=-1, keepdims=True) / channels + norm_eps)
+
+
+def pick_column(table):
+    lanes = lax.broadcasted_iota(jnp.int32, table.shape, 1)
+    return jnp.sum(jnp.where(lanes == pl.program_id(0), table, 0.0), axis=-1, keepdims=True)
+
+
+def gate_terms(act, weight):
+    gate_pre = dot(act, weight)
+    gate_sig = jax.nn.sigmoid(gate_pre)
+    return gate_pre, gate_sig
+
+
+def enter_kernel(x_ref, gain_ref, inner_ref, twiddle_ref, act_ref, mixed_ref):
+    wide = x_ref[...].astype(jnp.float32)
+    act = (wide * row_scale(wide, wide.shape[1]) * gain_ref[...]).astype(jnp.bfloat16)
+    act_ref[...] = act
+    mixed = dot(inner_ref[...], act[:, : mixed_ref.shape[-1]]) * pick_column(twiddle_ref[...])
+    mixed_ref[...] = mixed.astype(jnp.bfloat16).reshape(mixed_ref.shape)
+
+
+def inner_kernel(act_ref, inner_ref, twiddle_ref, mixed_ref):
+    mixed = dot(inner_ref[...], act_ref[...]) * pick_column(twiddle_ref[...])
+    mixed_ref[...] = mixed.astype(jnp.bfloat16).reshape(mixed_ref.shape)
+
+
+def mix_grad_kernel(act_ref, cot_ref, gate_ref, out_ref, *grad_refs):
+    for k, ref in enumerate(grad_refs):
+        size = ref.shape[-1]
+        part = slice(k * size, (k + 1) * size)
+        gate_pre, gate_sig = gate_terms(act_ref[:, part], gate_ref[part, :])
+        back = dot(cot_ref[:, part], out_ref[part, :], 1, 1)
+        ref[...] = (back * gate_pre * gate_sig).astype(jnp.bfloat16).reshape(ref.shape)
+
+
+def gate_kernel(blocks, x_ref, act_ref, cot_ref, gate_ref, out_ref, *refs):
+    seq_refs = refs[:blocks]
+    layer_ref, grad_ref, term_ref = refs[blocks:]
+    size = gate_ref.shape[1]
+
+    @pl.when(pl.program_id(0) == 0)
+    def _():
+        term_ref[...] = jnp.zeros_like(term_ref)
+
+    for k, seq_ref in enumerate(seq_refs):
+        part = slice(k * size, (k + 1) * size)
+        act = act_ref[:, part]
+        cot = cot_ref[:, part]
+        gate_pre, gate_sig = gate_terms(act, gate_ref[part, :])
+        mix = seq_ref[...].reshape(act.shape).astype(jnp.float32)
+        gated = (mix * gate_pre * gate_sig).astype(jnp.bfloat16)
+        layer_ref[:, part] = (
+            x_ref[:, part].astype(jnp.float32) + dot(gated, out_ref[part, :])
+        ).astype(jnp.bfloat16)
+        back = dot(cot, out_ref[part, :], 1, 1)
+        grad = (back * mix * gate_sig * (1.0 + gate_pre * (1.0 - gate_sig))).astype(jnp.bfloat16)
+        grad_ref[:, part] = grad
+        term_ref[part, :] += dot(act, grad, 0, 0)
+        low = (blocks + k) * size
+        term_ref[low : low + size, :] += dot(gated, cot, 0, 0)
+
+
+def leave_kernel(
+    blocks, x_ref, cot_ref, grad_ref, gain_ref, inner_t_ref, twiddle_ref, gate_t_ref, *refs
+):
+    back_refs = refs[:blocks]
+    result_ref = refs[blocks]
+    size = gate_t_ref.shape[1]
+    column = pick_column(twiddle_ref[...])
+    parts = []
+    for k, back_ref in enumerate(back_refs):
+        part = slice(k * size, (k + 1) * size)
+        rows = back_ref[...].reshape(x_ref.shape[0], size).astype(jnp.float32)
+        twisted = (rows * column).astype(jnp.bfloat16)
+        parts.append(
+            dot(grad_ref[:, part], gate_t_ref[part, :]) + dot(inner_t_ref[...], twisted)
+        )
+    act_grad = jnp.concatenate(parts, axis=1)
+    wide = x_ref[...].astype(jnp.float32)
+    scale = row_scale(wide, wide.shape[1])
+    pulled = act_grad * gain_ref[...]
+    share = jnp.sum(pulled * wide, axis=-1, keepdims=True) / wide.shape[1]
+    grad = pulled * scale - wide * (scale * scale * scale * share)
+    result_ref[...] = (cot_ref[...].astype(jnp.float32) + grad).astype(jnp.bfloat16)
+
+
+def shards_fast(
+    inputs,
+    norm_gain,
+    inner_mix,
+    twiddle,
+    outer_mix,
+    long_kernel,
+    gate_weight,
+    out_weight,
+    cotangent,
+):
+    batch, rows_local, channels = inputs.shape
+    inner_len = inner_mix.shape[0]
+    outer_len = outer_mix.shape[0]
+    local_outer = rows_local // inner_len
+    flat = batch * rows_local
+    steps = batch * local_outer
+    size = gate_weight.shape[1]
+    blocks = gate_weight.shape[0] // size
+    seq_n = lax.axis_size("seq")
+    dp_n = lax.axis_size("dp")
+    cols = inner_len // seq_n
+    grad_scale = 1.0 / math.sqrt(batch * dp_n * rows_local * seq_n)
+    bf16 = jnp.bfloat16
+
+    x = inputs.reshape(flat, channels)
+    cot = cotangent.reshape(flat, channels)
+    gain = norm_gain.reshape(1, channels)
+    twiddle_cols = jnp.tile(twiddle.T, (1, batch))
+    inner_t = inner_mix.T
+    gate_t = gate_weight.reshape(blocks, size, size).swapaxes(1, 2).reshape(blocks * size, size)
+
+    row_spec = pl.BlockSpec((inner_len, channels), lambda r: (r, 0))
+    swap_spec = pl.BlockSpec((seq_n, 1, cols, size), lambda r: (0, r, 0, 0))
+    row_shape = jax.ShapeDtypeStruct((flat, channels), bf16)
+    swap_shape = jax.ShapeDtypeStruct((seq_n, steps, cols, size), bf16)
+
+    def whole(array):
+        return pl.BlockSpec(array.shape, lambda r: (0,) * array.ndim)
+
+    def cost(matmuls, arrays):
+        return pl.CostEstimate(
+            flops=2 * flat * channels * matmuls,
+            bytes_accessed=int(2 * flat * channels * arrays),
+            transcendentals=0,
+        )
+
+    def exchange(held):
+        return lax.all_to_all(held, "seq", split_axis=0, concat_axis=0, tiled=True)
+
+    act, first = pl.pallas_call(
+        enter_kernel,
+        grid=(steps,),
+        in_specs=[row_spec, whole(gain), whole(inner_mix), whole(twiddle_cols)],
+        out_specs=[row_spec, swap_spec],
+        out_shape=[row_shape, swap_shape],
+        cost_estimate=cost(inner_len // blocks, 2.5),
+        name="enter",
+    )(x, gain, inner_mix, twiddle_cols)
+    columns = [exchange(first)]
+    for k in range(1, blocks):
+        mixed = pl.pallas_call(
+            inner_kernel,
+            grid=(steps,),
+            in_specs=[
+                pl.BlockSpec((inner_len, size), functools.partial(lambda k, r: (r, k), k)),
+                whole(inner_mix),
+                whole(twiddle_cols),
+            ],
+            out_specs=swap_spec,
+            out_shape=swap_shape,
+            cost_estimate=cost(inner_len // blocks, 1),
+            name="inner",
+        )(act, inner_mix, twiddle_cols)
+        columns.append(exchange(mixed))
+
+    mix_grad = pl.pallas_call(
+        mix_grad_kernel,
+        grid=(steps,),
+        in_specs=[row_spec, row_spec, whole(gate_weight), whole(out_weight)],
+        out_specs=[swap_spec] * blocks,
+        out_shape=[swap_shape] * blocks,
+        cost_estimate=cost(2 * size, 3),
+        name="mix_grad",
+    )(act, cot, gate_weight, out_weight)
+    grad_cols = [exchange(part) for part in mix_grad]
+
+    by_column = (seq_n, batch, local_outer, cols, size)
+
+    def gather_outer(part):
+        return part.reshape(by_column).swapaxes(0, 1).reshape(batch, outer_len, cols, size)
+
+    def split_outer(part):
+        part = part.reshape(batch, seq_n, local_outer, cols, size).swapaxes(0, 1)
+        return part.reshape(seq_n, steps, cols, size)
+
+    def outer_forward(part):
+        out = jnp.einsum(
+            "ip,bpjd->bijd", outer_mix, gather_outer(part), preferred_element_type=jnp.float32
+        )
+        return split_outer((out * long_kernel[None, :, :, None]).astype(bf16))
+
+    def outer_backward(part):
+        wide = gather_outer(part).astype(jnp.float32)
+        scaled = (wide * long_kernel[None, :, :, None]).astype(bf16)
+        out = jnp.einsum("ip,bijd->bpjd", outer_mix, scaled, preferred_element_type=jnp.float32)
+        return split_outer(out.astype(bf16))
+
+    seq_mix = [exchange(outer_forward(part)) for part in columns]
+    back_rows = [exchange(outer_backward(part)) for part in grad_cols]
+
+    term_rows = 2 * blocks * size
+    layer_out, gate_grad, term = pl.pallas_call(
+        functools.partial(gate_kernel, blocks),
+        grid=(steps,),
+        in_specs=[row_spec] * 3 + [whole(gate_weight), whole(out_weight)] + [swap_spec] * blocks,
+        out_specs=[row_spec, row_spec, pl.BlockSpec((term_rows, size), lambda r: (0, 0))],
+        out_shape=[row_shape, row_shape, jax.ShapeDtypeStruct((term_rows, size), jnp.float32)],
+        cost_estimate=cost(5 * size, 6),
+        name="gate",
+    )(x, act, cot, gate_weight, out_weight, *seq_mix)
+
+    piece = term_rows // seq_n // dp_n
+    term = term.reshape(seq_n, dp_n, piece, size).swapaxes(0, 1)
+    term = term.reshape(dp_n * seq_n * piece, size)
+    term = lax.psum_scatter(term, "dp", scatter_dimension=0, tiled=True)
+    term = lax.psum_scatter(term, "seq", scatter_dimension=0, tiled=True)
+    weight_grads = lax.all_gather(term * grad_scale, "dp", axis=0, tiled=True)
+
+    input_grad = pl.pallas_call(
+        functools.partial(leave_kernel, blocks),
+        grid=(steps,),
+        in_specs=[row_spec] * 3
+        + [whole(gain), whole(inner_t), whole(twiddle_cols), whole(gate_t)]
+        + [swap_spec] * blocks,
+        out_specs=row_spec,
+        out_shape=row_shape,
+        cost_estimate=cost(size + inner_len, 5),
+        name="leave",
+    )(x, cot, gate_grad, gain, inner_t, twiddle_cols, gate_t, *back_rows)
+    return (layer_out.reshape(inputs.shape), input_grad.reshape(inputs.shape), weight_grads)
+
+
+def shards(*arrays):
+    cols = arrays[5].shape[1]
+    pieces = 2 * arrays[6].shape[0] // lax.axis_size("seq") // lax.axis_size("dp")
+    if cols % 16 == 0 and pieces % 8 == 0:
+        return shards_fast(*arrays)
+    return shards_plain(*arrays)
+
+
 def solution(mesh):
     return jax.shard_map(
         shards,

time: 1650 us -> 1280 us (0.78)
  local copies, waits for them, and re-layouts: 327 us -> 34.5 us
  Pallas kernels: 0 us -> 186 us
  matrix products: 197 us -> 35.3 us
  other arithmetic: 117 us -> 9.83 us
  waiting for transfers between devices: 680 us -> 643 us
  starting transfers between devices: 27 us -> 48.9 us
  blocking collectives: 276 us -> 296 us
    pallas_call x0 -> x5, Pallas kernels: none -> 186 us  [the longest x1 65.2 us: shards_fast(): pl.pallas_call(functools.partial(gate_kernel, blocks), grid=(steps,), in_...]
    reduce_scatter x1 -> x2, waiting for transfers between devices: 205 us -> 34.7 us  [the longest x1 34.7 us: shards_fast(): term = lax.psum_scatter(term, 'dp', scatter_dimension=0, tiled=True)]
    dot_general x10 -> x4, matrix products: 197 us -> 35.3 us  [the longest x2 22.8 us: outer_backward(): jnp.einsum('ip,bijd->bpjd', outer_mix, scaled, preferred_element_type=jnp...]
    convert_element_type x11 -> x4, local copies, waits for them, and re-layouts: 186 us -> 25.7 us  [the longest x2 12.9 us: outer_backward(): return split_outer(out.astype(bf16))]
    all_to_all x3 -> x6, waiting for transfers between devices: 476 us -> 609 us  [exchange(): return lax.all_to_all(held, 'seq', split_axis=0, concat_axis=0, tiled=True)]
    convert_element_type x6 -> x2, other arithmetic: 85.6 us -> 8.91 us  [outer_backward(): wide = gather_outer(part).astype(jnp.float32)]
    reshape x3 -> x2, local copies, waits for them, and re-layouts: 74.1 us -> 2.35 us  [the longest x1 1.28 us: shards_fast(): gain = norm_gain.reshape(1, channels)]
    all_to_all x3 -> x0, local copies, waits for them, and re-layouts: 30.7 us -> none  [to_columns(): lax.all_to_all(row_layout, 'seq', split_axis=2, concat_axis=1, tiled=True)]
  transfers between devices with their start and end apart: 5 -> 8, of which waited for: 3 -> 7; matrix products, arithmetic and copies ran while one was open for 12% -> 6% of each run, Pallas kernels for 0% -> 11%
where the time goes in v1:
time: 1280 us; the launch traced here: 1270 us
  waiting for transfers between devices  643 us (50%)
  blocking collectives  296 us (23%)
  Pallas kernels  186 us (15%)
  starting transfers between devices  48.9 us (4%)
  matrix products  35.3 us (3%)
  local copies, waits for them, and re-layouts  34.5 us (3%)
  between operations  14.4 us (1%)
    all_to_all x6, waiting for transfers between devices, exchange(): return lax.all_to_all(held, 'seq', split_axis=0, concat_axis=0, tiled=True)  609 us
    all_to_all x2, blocking collectives, exchange(): return lax.all_to_all(held, 'seq', split_axis=0, concat_axis=0, tiled=True)  287 us
    pallas_call x1, Pallas kernels, shards_fast(): pl.pallas_call(functools.partial(gate_kernel, blocks), grid=(steps,), in_...  65.2 us
    all_to_all x6, starting transfers between devices, exchange(): return lax.all_to_all(held, 'seq', split_axis=0, concat_axis=0, tiled=True)  48.9 us
    pallas_call x1, Pallas kernels, shards_fast(): pl.pallas_call(functools.partial(leave_kernel, blocks), grid=(steps,), in...  40.2 us
    reduce_scatter x1, waiting for transfers between devices, shards_fast(): term = lax.psum_scatter(term, 'dp', scatter_dimension=0, tiled=True)  34.7 us
    pallas_call x1, Pallas kernels, shards_fast(): pl.pallas_call(mix_grad_kernel, grid=(steps,), in_specs=[row_spec, row_sp...  33.6 us
  transfers between devices with their start and end apart: 8, of which 7 were waited for; matrix products, arithmetic and copies ran while one was open for 6% of the time, Pallas kernels for 11%

profile of v1, /device:TPU:21, one launch (start us, length us, event | category | flops | bytes accessed | tf_op | source)
XLA Modules:
  0.0 1267.4 jit_solution(15910011745326725907)
XLA Ops:
  10.0 25.1 %enter.1 = (bf16[8192,768]{1,0:T(8,128)(2,1)}, bf16[4,32,64,384]{3,2,1,0:T(8,128)(2,1)}) custom-call(bf16[8192,768]{1,0:T(8,128)(2,1)} %bitcast.57, f32[1,768]{1,0:T(1,128)} %reshape.69.gain_ref, bf16[256,256]{1,0:T(8,128)(2,1)} %inner_ref.3, f32[256,32]{1,0:T(8,128)} %bitcast.72), custom_call_target="tpu_custom_call" | custom-call | flops 1610612736 | bytes 31457280 | tf_op jit(solution)/shard_map/enter/pallas_call | solution.py:261
  35.0 21.5 %inner.1 = bf16[4,32,64,384]{3,2,1,0:T(8,128)(2,1)} custom-call(bf16[8192,768]{1,0:T(8,128)(2,1)} %get-tuple-element.10.act_ref, bf16[256,256]{1,0:T(8,128)(2,1)} %inner_ref.3, f32[256,32]{1,0:T(8,128)} %bitcast.73), custom_call_target="tpu_custom_call" | custom-call | flops 1610612736 | bytes 12582912 | tf_op jit(solution)/shard_map/inner/pallas_call | solution.py:272
  56.5 141.9 %all_to_all.40 = bf16[4,32,64,384]{3,2,1,0:T(8,128)(2,1)} all-to-all(bf16[4,32,64,384]{3,2,1,0:T(8,128)(2,1)} %inner.1), channel_id=1, replica_groups=mesh['groups'=2,'seq'=4,'dp'=4] {'seq'}, dimensions={0} | all-to-all | bytes 12582912 | tf_op jit(solution)/shard_map/all_to_all | solution.py:259
  198.4 7.4 all-to-all-start
  205.8 33.6 %mix_grad.1 = (bf16[4,32,64,384]{3,2,1,0:T(8,128)(2,1)}, bf16[4,32,64,384]{3,2,1,0:T(8,128)(2,1)}) custom-call(bf16[8192,768]{1,0:T(8,128)(2,1)} %get-tuple-element.10.act_ref, bf16[8192,768]{1,0:T(8,128)(2,1)} %bitcast.65, bf16[768,384]{1,0:T(8,128)(2,1)} %gate_ref.3, bf16[768,384]{1,0:T(8,128)(2,1)} %out_ref.3), custom_call_target="tpu_custom_call" | custom-call | flops 9663676416 | bytes 37748736 | tf_op jit(solution)/shard_map/mix_grad/pallas_call | solution.py:287
  239.4 101.1 %all-to-all-done = bf16[4,32,64,384]{3,2,1,0:T(8,128)(2,1)} async-done(((bf16[4,32,64,384]{3,2,1,0:T(8,128)(2,1)}), bf16[4,32,64,384]{3,2,1,0:T(8,128)(2,1)}, u32[]{:S(2)}, u32[]{:S(2)}) %all-to-all-start) | async-done | bytes 6291488 | tf_op jit(solution)/shard_map/all_to_all | solution.py:259
  340.4 145.0 %all_to_all.41 = bf16[4,32,64,384]{3,2,1,0:T(8,128)(2,1)} all-to-all(bf16[4,32,64,384]{3,2,1,0:T(8,128)(2,1)} %get-tuple-element.14), channel_id=1, replica_groups=mesh['groups'=2,'seq'=4,'dp'=4] {'seq'}, dimensions={0} | all-to-all | bytes 12582912 | tf_op jit(solution)/shard_map/all_to_all | solution.py:259
  485.4 7.3 all-to-all-start.6
  505.4 122.0 %all-to-all-done.6 = bf16[4,32,64,384]{3,2,1,0:T(8,128)(2,1)} async-done(((bf16[4,32,64,384]{3,2,1,0:T(8,128)(2,1)}), bf16[4,32,64,384]{3,2,1,0:T(8,128)(2,1)}, u32[]{:S(2)}, u32[]{:S(2)}) %all-to-all-start.6) | async-done | bytes 6291488 | tf_op jit(solution)/shard_map/all_to_all | solution.py:259
  627.4 8.8 all-to-all-start.3
  642.5 6.5 copy.14
  648.9 121.9 %all-to-all-done.3.refs_1_ = bf16[4,32,64,384]{3,2,1,0:T(8,128)(2,1)} async-done(((bf16[4,32,64,384]{3,2,1,0:T(8,128)(2,1)}), bf16[4,32,64,384]{3,2,1,0:T(8,128)(2,1)}, u32[]{:S(2)}, u32[]{:S(2)}) %all-to-all-start.3) | async-done | bytes 6291488 | tf_op jit(solution)/shard_map/all_to_all | solution.py:259
  770.8 8.5 all-to-all-start.1
  783.7 11.4 convert_bitcast_fusion.1
  801.6 112.3 %all-to-all-done.1.refs_0_ = bf16[4,32,64,384]{3,2,1,0:T(8,128)(2,1)} async-done(((bf16[4,32,64,384]{3,2,1,0:T(8,128)(2,1)}), bf16[4,32,64,384]{3,2,1,0:T(8,128)(2,1)}, u32[]{:S(2)}, u32[]{:S(2)}) %all-to-all-start.1) | async-done | bytes 6291488 | tf_op jit(solution)/shard_map/all_to_all | solution.py:259
  913.9 8.5 all-to-all-start.5
  926.9 11.4 convert_bitcast_fusion
  944.8 112.3 %all-to-all-done.5.refs_0_ = bf16[4,32,64,384]{3,2,1,0:T(8,128)(2,1)} async-done(((bf16[4,32,64,384]{3,2,1,0:T(8,128)(2,1)}), bf16[4,32,64,384]{3,2,1,0:T(8,128)(2,1)}, u32[]{:S(2)}, u32[]{:S(2)}) %all-to-all-start.5) | async-done | bytes 6291488 | tf_op jit(solution)/shard_map/all_to_all | solution.py:259
  1057.1 8.4 all-to-all-start.7
  1065.5 65.2 %gate.1 = (bf16[8192,768]{1,0:T(8,128)(2,1)}, bf16[8192,768]{1,0:T(8,128)(2,1)}, f32[1536,384]{1,0:T(8,128)}) custom-call(bf16[8192,768]{1,0:T(8,128)(2,1)} %bitcast.58, bf16[8192,768]{1,0:T(8,128)(2,1)} %get-tuple-element.10.act_ref, bf16[8192,768]{1,0:T(8,128)(2,1)} %bitcast.66, bf16[768,384]{1,0:T(8,128)(2,1)} %gate_ref.3, bf16[768,384]{1,0:T(8,128)(2,1)} %out_ref.3, ...), custom_call_target="tpu_custom_call" | custom-call | flops 24159191040 | bytes 75497472 | tf_op jit(solution)/shard_map/gate/pallas_call | solution.py:323
  1134.1 34.7 %reduce-scatter.3.cloned.1.call-done = f32[384,384]{1,0:T(8,128)} async-done(((f32[1536,384]{1,0:T(8,128)}), f32[384,384]{1,0:T(8,128)}) %reduce-scatter.3.cloned.1.call-update) | async-done | bytes 589840 | tf_op jit(solution)/shard_map/reduce_scatter | solution.py:336
  1170.6 39.0 %all-to-all-done.7.refs_1_ = bf16[4,32,64,384]{3,2,1,0:T(8,128)(2,1)} async-done(((bf16[4,32,64,384]{3,2,1,0:T(8,128)(2,1)}), bf16[4,32,64,384]{3,2,1,0:T(8,128)(2,1)}, u32[]{:S(2)}, u32[]{:S(2)}) %all-to-all-start.7) | async-done | bytes 6291488 | tf_op jit(solution)/shard_map/all_to_all | solution.py:259
  1209.6 40.2 %leave.1 = bf16[8192,768]{1,0:T(8,128)(2,1)} custom-call(bf16[8192,768]{1,0:T(8,128)(2,1)} %bitcast.59, bf16[8192,768]{1,0:T(8,128)(2,1)} %bitcast.67, bf16[8192,768]{1,0:T(8,128)(2,1)} %get-tuple-element.13.grad_ref, f32[1,768]{1,0:T(1,128)} %reshape.69.gain_ref, bf16[256,256]{1,0:T(8,128)(2,1)} %bitcast.76, f32[256,32]{1,0:T(8,128)} %bitcast.74, ...), custom_call_target="tpu_custom_call" | custom-call | flops 8053063680 | bytes 62914560 | tf_op jit(solution)/shard_map/leave/pallas_call | solution.py:340
  1250.8 8.8 all_gather.3
  (29 shorter events, 50.5 us)
Async XLA Ops:
  7.2 485.6 %copy-start = (bf16[128,128]{1,0:T(8,128)(2,1)S(1)}, bf16[128,128]{1,0:T(8,128)(2,1)}, u32[]{:S(2)}) copy-start(bf16[128,128]{1,0:T(8,128)(2,1)} %param.13) | copy-start | bytes 98308
  198.4 142.0 %all-to-all-start = ((bf16[4,32,64,384]{3,2,1,0:T(8,128)(2,1)}), bf16[4,32,64,384]{3,2,1,0:T(8,128)(2,1)}, u32[]{:S(2)}, u32[]{:S(2)}) async-start(bf16[4,32,64,384]{3,2,1,0:T(8,128)(2,1)} %get-tuple-element.11), calls=%async_computation | async-start | bytes 12582912 | tf_op jit(solution)/shard_map/all_to_all | solution.py:259
  485.4 7.4 copy-start.4
  485.4 142.0 %all-to-all-start.6 = ((bf16[4,32,64,384]{3,2,1,0:T(8,128)(2,1)}), bf16[4,32,64,384]{3,2,1,0:T(8,128)(2,1)}, u32[]{:S(2)}, u32[]{:S(2)}) async-start(bf16[4,32,64,384]{3,2,1,0:T(8,128)(2,1)} %get-tuple-element.15), calls=%async_computation.6 | async-start | bytes 12582912 | tf_op jit(solution)/shard_map/all_to_all | solution.py:259
  627.4 143.4 %all-to-all-start.3 = ((bf16[4,32,64,384]{3,2,1,0:T(8,128)(2,1)}), bf16[4,32,64,384]{3,2,1,0:T(8,128)(2,1)}, u32[]{:S(2)}, u32[]{:S(2)}) async-start(bf16[4,32,64,384]{3,2,1,0:T(8,128)(2,1)} %bitcast.64), calls=%async_computation.3 | async-start | bytes 12582912 | tf_op jit(solution)/shard_map/all_to_all | solution.py:259
  770.8 143.1 %all-to-all-start.1 = ((bf16[4,32,64,384]{3,2,1,0:T(8,128)(2,1)}), bf16[4,32,64,384]{3,2,1,0:T(8,128)(2,1)}, u32[]{:S(2)}, u32[]{:S(2)}) async-start(bf16[4,32,64,384]{3,2,1,0:T(8,128)(2,1)} %bitcast.62), calls=%async_computation.1 | async-start | bytes 12582912 | tf_op jit(solution)/shard_map/all_to_all | solution.py:259
  913.9 143.2 %all-to-all-start.5 = ((bf16[4,32,64,384]{3,2,1,0:T(8,128)(2,1)}), bf16[4,32,64,384]{3,2,1,0:T(8,128)(2,1)}, u32[]{:S(2)}, u32[]{:S(2)}) async-start(bf16[4,32,64,384]{3,2,1,0:T(8,128)(2,1)} %bitcast.63), calls=%async_computation.5 | async-start | bytes 12582912 | tf_op jit(solution)/shard_map/all_to_all | solution.py:259
  1057.1 152.5 %all-to-all-start.7 = ((bf16[4,32,64,384]{3,2,1,0:T(8,128)(2,1)}), bf16[4,32,64,384]{3,2,1,0:T(8,128)(2,1)}, u32[]{:S(2)}, u32[]{:S(2)}) async-start(bf16[4,32,64,384]{3,2,1,0:T(8,128)(2,1)} %bitcast.60), calls=%async_computation.7 | async-start | bytes 12582912 | tf_op jit(solution)/shard_map/all_to_all | solution.py:259
  1065.5 103.3 %reduce-scatter.3.cloned.1.call-start = ((), (), s32[]{:S(2)}) async-start(), calls=%async_computation.10 | async-start | bytes 2949120 | tf_op jit(solution)/shard_map/reduce_scatter | solution.py:336
  1130.7 38.1 %copy-start.2 = (bf16[256,256]{1,0:T(8,128)(2,1)S(1)}, bf16[256,256]{1,0:T(8,128)(2,1)}, u32[]{:S(2)}) copy-start(bf16[256,256]{1,0:T(8,128)(2,1)} %inner_ref.3) | copy-start | bytes 393220
  1130.7 38.8 %copy-start.3 = (bf16[768,384]{1,0:T(8,128)(2,1)S(1)}, bf16[768,384]{1,0:T(8,128)(2,1)}, u32[]{:S(2)}) copy-start(bf16[768,384]{1,0:T(8,128)(2,1)} %gate_ref.3) | copy-start | bytes 1769476
  1134.1 115.8 %reduce-scatter.5.cloned.1.call-start = ((), (), s32[]{:S(2)}) async-start(), calls=%async_computation.11 | async-start | bytes 737280 | tf_op jit(solution)/shard_map/reduce_scatter | solution.py:337
  1209.6 50.8 %copy-start.1 = (bf16[128,128]{1,0:T(8,128)(2,1)S(1)}, bf16[128,128]{1,0:T(8,128)(2,1)}, u32[]{:S(2)}) copy-start(bf16[128,128]{1,0:T(8,128)(2,1)} %param.13) | copy-start | bytes 98308
Sparse Core Ops, SparseCore 0:
  1134.2 34.5 reduce-scatter.2
  1171.0 22.2 reduce-scatter.4
